TPU v7x, 256 devices: a whole 4x4x8 slice. The times are simulated.
256 devices in a mesh: group: 16 (over y, x), member: 16 (over z, core).
Axes of the slice: x: 4, y: 4, z: 8, core: 2. Of those that a mesh axis runs over, the one named last changes fastest.
Arguments:
- factor: float32 [16, 32, 768, 768], P('group', 'member'), as said below
- load: float32 [16, 32, 768], P('group', 'member'), may hold values from -6 to 6
- dof_map: int32 [16, 32, 768], P('group', 'member'), may hold values from 0 to 767, as said below
- dof_sign: int32 [16, 32, 768], P('group', 'member'), may hold values from -1 to 1, as said below
- live_count: int32 [16, 32], P('group', 'member'), may hold values from 384 to 768, as said below
- face_slot: int32 [16, 32, 4, 64], P('group', 'member'), may hold values from 0 to 767, as said below
- face_count: int32 [16, 32, 4], P('group', 'member'), may hold values from 0 to 64, as said below
- node_coord: int32 [16, 32, 3, 256], P('group', 'member'), may hold values from 0 to 15
- coarse_inverse: float32 [3072, 3072], P(('group', 'member')), as said below
Outputs:
- multipliers: float32 [16, 32, 768], P('group', 'member')
- projected: float32 [16, 32, 768], P('group', 'member')
Inputs may be any that keep to these rules, and one draw needn't show every extreme that they name: `dof_map`: each subdomain's row is a permutation of the unknowns. `dof_sign`: every entry is -1 or 1. `live_count`: in each cluster, both subdomains of one device have 768 live multipliers and both subdomains of the device whose member index differs by a quarter of 32 have 384. `face_slot`: the slots of one subdomain are distinct and below its live_count; slot k of a face pairs with slot k of the partner's face. `face_count`: A face and its partner's face have the same count; faces at the ends of a cluster's chain and at the first and last cluster have 0, all others 1 or more. `factor`: lower triangular with a positive diagonal. `coarse_inverse`: symmetric positive definite.
All inputs are finite; a program needn't handle non-finite values.
Results may differ from a plain program's by a relative error of at most 0.0003.
Values sent between devices are 32-bit elements; how exact they have to be, the bound alone decides.
No kernel may reach another device: no remote copies, remote signals or barrier semaphores. Data moves between devices by JAX's collectives and lax.ppermute only.
A program may use at most 128 MiB of HBM per device.

v0:
```python
import math
import jax
import jax.numpy as jnp
from jax import lax
from jax.sharding import PartitionSpec as P

ITERS = 3
highest = lax.Precision.HIGHEST
half_span = 8.0


def from_partner(value, axis, bit):
    mask = 2**bit
    pairs = [(source, source ^ mask) for source in range(lax.axis_size(axis))]
    return lax.ppermute(value, axis, pairs)


def padded(array, sides, width):
    for axis, dim in sides:
        size, length = (lax.axis_size(axis), array.shape[dim])
        up = [(i, (i + 1) % size) for i in range(size - 1)]
        down = [(j, i) for i, j in up]
        last = lax.slice_in_dim(array, length - width, length, axis=dim)
        leading = lax.slice_in_dim(array, 0, width, axis=dim)
        before = lax.ppermute(last, axis, up)
        after = lax.ppermute(leading, axis, down)
        array = jnp.concatenate([before, array, after], axis=dim)
    return array


def rigid_modes(node_coord):
    position = (node_coord.astype(jnp.float32) - half_span) / half_span
    spread = jnp.repeat(position, 3, axis=-1)
    component = jnp.arange(spread.shape[-1], dtype=jnp.int32) % 3
    first = (component == 0).astype(spread.dtype)
    second = (component == 1).astype(spread.dtype)
    third = (component == 2).astype(spread.dtype)
    coord_x = spread[..., 0, :]
    coord_y = spread[..., 1, :]
    coord_z = spread[..., 2, :]
    unit_row = jnp.ones_like(coord_x)
    return jnp.stack(
        [
            first * unit_row,
            second * unit_row,
            third * unit_row,
            third * coord_y - second * coord_z,
            first * coord_z - third * coord_x,
            second * coord_x - first * coord_y,
        ],
        axis=-2,
    )


def lower_solve(panel_matrix, right_side):
    return lax.linalg.triangular_solve(panel_matrix, right_side, left_side=True, lower=True)


def upper_solve(panel_matrix, right_side):
    return lax.linalg.triangular_solve(
        panel_matrix, right_side, left_side=True, lower=True, transpose_a=True
    )


def dual_of(panel_matrix, dof_codes, block_count, block_width):
    dof_count = panel_matrix.shape[0]
    slot_total = dof_codes.shape[0]
    levels = jnp.arange(dof_count, dtype=jnp.float32)[:, None]

    def solve_block(block_index, solved):
        columns = lax.dynamic_slice_in_dim(dof_codes, block_index * block_width, block_width)
        target = jnp.where(
            levels == jnp.abs(columns)[None, :] - 1.0, jnp.sign(columns)[None, :], 0.0
        )
        solved_piece = lower_solve(panel_matrix, target)
        return lax.dynamic_update_slice_in_dim(solved, solved_piece, block_index * block_width, 1)

    solved = lax.fori_loop(
        0, block_count, solve_block, jnp.zeros((dof_count, slot_total), jnp.float32)
    )

    def product_block(block_index, dual_sum):
        solved_piece = lax.dynamic_slice_in_dim(solved, block_index * block_width, block_width, 1)
        column = lax.dot_general(
            solved,
            solved_piece,
            (((0,), (0,)), ((), ())),
            precision=highest,
            preferred_element_type=jnp.float32,
        )
        return lax.dynamic_update_slice_in_dim(dual_sum, column, block_index * block_width, 1)

    return lax.fori_loop(
        0, block_count, product_block, jnp.zeros((slot_total, slot_total), jnp.float32)
    )


def shards(
    factor, load, dof_map, dof_sign, live_count, face_slot, face_count, node_coord, coarse_inverse
):
    own_panels = factor[0]
    own_loads = load[0]
    dof_count = own_loads.shape[1]
    subs_here = own_loads.shape[0]
    face_cap = face_slot.shape[3]
    block_width = math.gcd(dof_count, 128)
    positions = jnp.arange(dof_count, dtype=jnp.int32)
    live_mask = positions[None, :] < live_count[0][:, None]
    signed = jnp.where(live_mask, dof_sign[0], 0)
    dof_codes = ((dof_map[0] + 1) * signed).astype(jnp.float32)
    signed_float = signed.astype(jnp.float32)
    blocks_own = (live_count[0] + block_width - 1) // block_width
    bit_pos = lax.axis_size("member").bit_length() - 2
    partner_panel, partner_codes = from_partner((own_panels[1], dof_codes), "member", bit_pos)
    first_dual = dual_of(own_panels[0], dof_codes[0], blocks_own[0], block_width)
    partner_blocks = (
        jnp.sum((partner_codes != 0).astype(jnp.int32), axis=1) + block_width - 1
    ) // block_width
    upper_half = lax.axis_index("member") // (lax.axis_size("member") // 2) % 2 == 1
    lower_blocks = jnp.where(upper_half, partner_blocks, blocks_own)
    upper_blocks = jnp.where(upper_half, blocks_own, partner_blocks)
    lower_loads = jnp.stack(
        [
            lower_blocks[0] + lower_blocks[1],
            lower_blocks[0],
            lower_blocks[0] + lower_blocks[1] + upper_blocks[1],
            lower_blocks[0] + upper_blocks[1],
        ]
    )
    upper_loads = jnp.stack(
        [
            upper_blocks[0] + upper_blocks[1],
            upper_blocks[0] + upper_blocks[1] + lower_blocks[1],
            upper_blocks[0],
            upper_blocks[0] + lower_blocks[1],
        ]
    )
    option_pick = jnp.argmin(jnp.maximum(lower_loads, upper_loads))
    lower_moves = (option_pick == 1) | (option_pick == 3)
    upper_moves = (option_pick == 2) | (option_pick == 3)
    give_mine = jnp.where(upper_half, upper_moves, lower_moves)
    take_theirs = jnp.where(upper_half, lower_moves, upper_moves)
    kept_dual = dual_of(
        own_panels[1], dof_codes[1], jnp.where(give_mine, 0, blocks_own[1]), block_width
    )
    helped_dual = dual_of(
        partner_panel, partner_codes[1], jnp.where(take_theirs, partner_blocks[1], 0), block_width
    )
    returned = from_partner(helped_dual, "member", bit_pos)
    second_dual = jnp.where(give_mine, returned, kept_dual)
    dual_pair = jnp.stack([first_dual, second_dual])
    forward = jax.vmap(lambda panel_one, load_one: lower_solve(panel_one, load_one[:, None]))(
        own_panels, own_loads
    )
    displaced = jax.vmap(upper_solve)(own_panels, forward)[:, :, 0]
    gap_local = jnp.take_along_axis(displaced, dof_map[0], axis=1) * signed_float
    mode_table = rigid_modes(node_coord[0])
    rigid_rows = jnp.take_along_axis(
        mode_table, jnp.broadcast_to(dof_map[0][:, None, :], mode_table.shape), axis=2
    )
    rigid_rows = rigid_rows * signed_float[:, None, :]
    coarse_rhs = jnp.einsum("lai,li->la", mode_table, own_loads, precision=highest)
    slot_list = face_slot[0].reshape(subs_here, 4 * face_cap)
    slot_used = (
        jnp.arange(face_cap, dtype=jnp.int32)[None, None, :] < face_count[0][:, :, None]
    ).reshape(subs_here, 4 * face_cap)
    slot_table = (
        (slot_list[:, :, None] == positions[None, None, :]) & slot_used[:, :, None]
    ).astype(jnp.float32)
    shared = jnp.sum(slot_table, axis=1)
    weight = live_mask.astype(jnp.float32) * (1.0 - 0.5 * shared)

    def assemble(values):
        outgoing = jnp.einsum("lkj,lj->lk", slot_table, values, precision=highest)
        extended = padded(outgoing[None], (("group", 0), ("member", 1)), 1)
        incoming = jnp.stack(
            [
                jnp.concatenate(
                    [
                        extended[1, sub_index, face_cap : 2 * face_cap],
                        extended[1, sub_index + 2, 0:face_cap],
                        extended[0, sub_index + 1, 3 * face_cap : 4 * face_cap],
                        extended[2, sub_index + 1, 2 * face_cap : 3 * face_cap],
                    ]
                )
                for sub_index in range(subs_here)
            ]
        )
        return values + jnp.einsum("lk,lkj->lj", incoming, slot_table, precision=highest)

    def inner_part(left_field, right_field):
        return jnp.sum(weight * left_field * right_field)

    def global_sum(partial_value):
        return lax.psum(partial_value, ("group", "member"))

    def gather_coarse(local_coarse):
        return lax.all_gather(local_coarse.reshape(1, -1), ("group", "member"), axis=0, tiled=True)

    def coarse_of(values):
        return jnp.einsum("laj,lj->la", rigid_rows, values, precision=highest)

    def spread_modes(gathered):
        alpha = jnp.dot(coarse_inverse, gathered.reshape(-1), precision=highest).reshape(
            subs_here, -1
        )
        return assemble(jnp.einsum("laj,la->lj", rigid_rows, alpha, precision=highest))

    def apply_dual(values):
        return jnp.einsum("lij,lj->li", dual_pair, values, precision=highest)

    multipliers = spread_modes(gather_coarse(coarse_rhs))
    residual = assemble(gap_local - apply_dual(multipliers))
    coarse_res = gather_coarse(coarse_of(residual))
    projected = residual - spread_modes(coarse_res)
    direction = projected
    norm_now = global_sum(inner_part(projected, projected))
    for iteration in range(ITERS):
        image_vec = assemble(apply_dual(direction))
        curvature = global_sum(inner_part(direction, image_vec))
        step_size = norm_now / curvature
        multipliers = multipliers + step_size * direction
        residual = residual - step_size * image_vec
        coarse_res = gather_coarse(coarse_of(residual))
        projected = residual - spread_modes(coarse_res)
        norm_next = global_sum(inner_part(projected, projected))
        direction = projected + norm_next / norm_now * direction
        norm_now = norm_next
    return (multipliers[None], projected[None])


def solution(mesh):
    return jax.shard_map(
        shards,
        mesh=mesh,
        in_specs=(
            P("group", "member", None, None),
            P("group", "member", None),
            P("group", "member", None),
            P("group", "member", None),
            P("group", "member"),
            P("group", "member", None, None),
            P("group", "member", None),
            P("group", "member", None, None),
            P(("group", "member"), None),
        ),
        out_specs=(P("group", "member", None), P("group", "member", None)),
        check_vma=False,
    )
```

profile of v0, /device:TPU:15, one launch (start us, length us, event | category | flops | bytes accessed | tf_op | source)
XLA Modules:
  0.0 2192.2 jit_solution(2142416162315321795)
XLA Ops:
  4.6 71.1 %gather_fusion = f32[9216]{0:T(1024)S(1)} fusion(f32[2,6,768]{2,1,0:T(8,128)S(1)} %stack.144, s32[9216]{0:T(1024)S(1)} %reshape.418), kind=kCustom, calls=%fused_computation | custom fusion | bytes 184320 | tf_op jit(solution)/shard_map/jit(take_along_axis)/gather | solution.py:158
  75.9 58.2 %all-gather = f32[256,1,12]{2,1,0:T(1,128)S(1)} all-gather(f32[1,1,12]{2,1,0:T(1,128)S(1)} %reshape.430), channel_id=1, replica_groups=mesh['group'=16,'member'=16] {'group','member'}, dimensions={0}, use_global_device_ids=true | all-gather | bytes 12336 | tf_op jit(solution)/shard_map/all_gather | solution.py:198
  179.9 117.9 %custom-call.8 = f32[2,6,128,128]{2,3,1,0:T(8,128)S(1)} custom-call(f32[2,6,128,128]{3,2,1,0:T(8,128)S(1)} %bitcast.1018), custom_call_target="InvertDiagBlocksLowerTriangular" | custom-call | tf_op jit(solution)/shard_map/vmap()/triangular_solve | solution.py:60
  351.9 324.7 %while.88 = (s32[]{:T(128)}, f32[768,768]{1,0:T(8,128)}, s32[]{:T(128)}, f32[768]{0:T(1024)S(1)}, f32[768,768]{1,0:T(8,128)}, /*index=5*/s32[]{:T(128)}, s32[]{:T(128)}, s32[]{:T(128)}, s32[]{:T(128)}, s32[]{:T(128)}) while((s32[]{:T(128)}, f32[768,768]{1,0:T(8,128)}, s32[]{:T(128)}, f32[768]{0:T(1024)S(1)}, ...), condition=%wide.region_12.14_spmd.clone, body=%wide.region_11.13_spmd.clone.sunk | while | flops 530268544 | bytes 10424716 | solution.py:78
  369.2 59.8 %custom-call.57 = f32[6,128,128]{1,2,0:T(8,128)S(1)} custom-call(f32[6,128,128]{2,1,0:T(8,128)} %get-tuple-element.1070), custom_call_target="InvertDiagBlocksLowerTriangular" | custom-call | tf_op jit(solution)/shard_map/while/body/triangular_solve/custom-call.1 | solution.py:56
  450.3 59.8 %custom-call.57 = f32[6,128,128]{1,2,0:T(8,128)S(1)} custom-call(f32[6,128,128]{2,1,0:T(8,128)} %get-tuple-element.1070), custom_call_target="InvertDiagBlocksLowerTriangular" | custom-call | tf_op jit(solution)/shard_map/while/body/triangular_solve/custom-call.1 | solution.py:56
  531.4 59.8 %custom-call.57 = f32[6,128,128]{1,2,0:T(8,128)S(1)} custom-call(f32[6,128,128]{2,1,0:T(8,128)} %get-tuple-element.1070), custom_call_target="InvertDiagBlocksLowerTriangular" | custom-call | tf_op jit(solution)/shard_map/while/body/triangular_solve/custom-call.1 | solution.py:56
  612.6 59.8 %custom-call.57 = f32[6,128,128]{1,2,0:T(8,128)S(1)} custom-call(f32[6,128,128]{2,1,0:T(8,128)} %get-tuple-element.1070), custom_call_target="InvertDiagBlocksLowerTriangular" | custom-call | tf_op jit(solution)/shard_map/while/body/triangular_solve/custom-call.1 | solution.py:56
  681.2 84.4 %collective-permute-start.6 = (f32[768,768]{0,1:T(8,128)}, f32[768,768]{0,1:T(8,128)}, u32[]{:S(2)}, u32[]{:S(2)}) collective-permute-start(f32[768,768]{0,1:T(8,128)} %get-tuple-element.317), channel_id=1, source_target_pairs={{0,8},{1,9},{2,10},{3,11},{4,12},{5,13},{6,14},{7,15},{8,0},{9,1},... | collective-permute-start | bytes 7077896 | tf_op jit(solution)/shard_map/ppermute | solution.py:15
  767.2 496.1 %while.84 = (s32[]{:T(128)}, f32[768,768]{1,0:T(8,128)}, s32[]{:T(128)}, f32[768]{0:T(1024)S(1)}, f32[768,768]{1,0:T(8,128)}, /*index=5*/s32[]{:T(128)}, s32[]{:T(128)}, s32[]{:T(128)}, s32[]{:T(128)}, s32[]{:T(128)}) while((s32[]{:T(128)}, f32[768,768]{1,0:T(8,128)}, s32[]{:T(128)}, f32[768]{0:T(1024)S(1)}, f32[768,768]{1,0:T(8,128)}, ...), condition=%wide.region_2.4_spmd.clone, body=%wide.region_1.3_spmd.clone.sunk | while | flops 530268544 | bytes 10424716 | solution.py:78
  785.8 59.8 %custom-call.51 = f32[6,128,128]{1,2,0:T(8,128)S(1)} custom-call(f32[6,128,128]{2,1,0:T(8,128)} %get-tuple-element.1024), custom_call_target="InvertDiagBlocksLowerTriangular" | custom-call | tf_op jit(solution)/shard_map/while/body/triangular_solve/custom-call.1 | solution.py:56
  868.3 59.8 %custom-call.51 = f32[6,128,128]{1,2,0:T(8,128)S(1)} custom-call(f32[6,128,128]{2,1,0:T(8,128)} %get-tuple-element.1024), custom_call_target="InvertDiagBlocksLowerTriangular" | custom-call | tf_op jit(solution)/shard_map/while/body/triangular_solve/custom-call.1 | solution.py:56
  950.9 59.8 %custom-call.51 = f32[6,128,128]{1,2,0:T(8,128)S(1)} custom-call(f32[6,128,128]{2,1,0:T(8,128)} %get-tuple-element.1024), custom_call_target="InvertDiagBlocksLowerTriangular" | custom-call | tf_op jit(solution)/shard_map/while/body/triangular_solve/custom-call.1 | solution.py:56
  1033.5 59.8 %custom-call.51 = f32[6,128,128]{1,2,0:T(8,128)S(1)} custom-call(f32[6,128,128]{2,1,0:T(8,128)} %get-tuple-element.1024), custom_call_target="InvertDiagBlocksLowerTriangular" | custom-call | tf_op jit(solution)/shard_map/while/body/triangular_solve/custom-call.1 | solution.py:56
  1116.1 59.8 %custom-call.51 = f32[6,128,128]{1,2,0:T(8,128)S(1)} custom-call(f32[6,128,128]{2,1,0:T(8,128)} %get-tuple-element.1024), custom_call_target="InvertDiagBlocksLowerTriangular" | custom-call | tf_op jit(solution)/shard_map/while/body/triangular_solve/custom-call.1 | solution.py:56
  1198.6 59.8 %custom-call.51 = f32[6,128,128]{1,2,0:T(8,128)S(1)} custom-call(f32[6,128,128]{2,1,0:T(8,128)} %get-tuple-element.1024), custom_call_target="InvertDiagBlocksLowerTriangular" | custom-call | tf_op jit(solution)/shard_map/while/body/triangular_solve/custom-call.1 | solution.py:56
  1332.9 142.5 %all-gather.1 = f32[256,1,12]{2,1,0:T(1,128)S(1)} all-gather(f32[1,1,12]{2,1,0:T(1,128)S(1)} %reshape.432), channel_id=1, replica_groups=mesh['group'=16,'member'=16] {'group','member'}, dimensions={0}, use_global_device_ids=true | all-gather | bytes 12336 | tf_op jit(solution)/shard_map/all_gather | solution.py:198
  1521.2 76.7 %all-reduce = (f32[]{:T(128)}, f32[]{:T(128)}) all-reduce(f32[]{:T(128)} %get-tuple-element.439, f32[]{:T(128)} %get-tuple-element.438), channel_id=1, replica_groups=mesh['group'=16,'member'=16] {'group','member'}, use_global_device_ids=true, to_apply=%region_16.18 | all-reduce | flops 2 | bytes 16 | tf_op jit(solution)/shard_map/psum | solution.py:195
  1678.0 74.4 %psum.44 = f32[]{:T(128)} all-reduce(f32[]{:T(128)} %fusion.217), channel_id=1, replica_groups=mesh['group'=16,'member'=16] {'group','member'}, use_global_device_ids=true, to_apply=%region_20.22 | all-reduce | flops 1 | bytes 8 | tf_op jit(solution)/shard_map/psum | solution.py:195
  1778.7 75.6 %psum.45 = f32[]{:T(128)} all-reduce(f32[]{:T(128)} %multiply_reduce_fusion.1), channel_id=1, replica_groups=mesh['group'=16,'member'=16] {'group','member'}, use_global_device_ids=true, to_apply=%region_22.24 | all-reduce | flops 1 | bytes 8 | tf_op jit(solution)/shard_map/psum | solution.py:195
  1855.9 54.4 %all-gather.3 = f32[256,1,12]{2,1,0:T(1,128)S(1)} all-gather(f32[1,1,12]{2,1,0:T(1,128)S(1)} %reshape.436), channel_id=1, replica_groups=mesh['group'=16,'member'=16] {'group','member'}, dimensions={0}, use_global_device_ids=true | all-gather | bytes 12336 | tf_op jit(solution)/shard_map/all_gather | solution.py:198
  1935.1 73.6 %psum.46 = f32[]{:T(128)} all-reduce(f32[]{:T(128)} %get-tuple-element.530), channel_id=1, replica_groups=mesh['group'=16,'member'=16] {'group','member'}, use_global_device_ids=true, to_apply=%region_24.26 | all-reduce | flops 1 | bytes 8 | tf_op jit(solution)/shard_map/psum | solution.py:195
  2035.8 74.8 %psum.47 = f32[]{:T(128)} all-reduce(f32[]{:T(128)} %multiply_reduce_fusion), channel_id=1, replica_groups=mesh['group'=16,'member'=16] {'group','member'}, use_global_device_ids=true, to_apply=%region_26.28 | all-reduce | flops 1 | bytes 8 | tf_op jit(solution)/shard_map/psum | solution.py:195
  2112.2 54.2 %all-gather.4 = f32[256,1,12]{2,1,0:T(1,128)S(1)} all-gather(f32[1,1,12]{2,1,0:T(1,128)S(1)} %reshape.438), channel_id=1, replica_groups=mesh['group'=16,'member'=16] {'group','member'}, dimensions={0}, use_global_device_ids=true | all-gather | bytes 12336 | tf_op jit(solution)/shard_map/all_gather | solution.py:198
  (781 shorter events, 819.0 us)
Async XLA Ops:
  138.7 190.5 %collective-permute-start = (f32[1,2,256]{2,1,0:T(2,128)S(1)}, f32[1,2,256]{2,1,0:T(2,128)S(1)}, u32[]{:S(2)}, u32[]{:S(2)}) collective-permute-start(f32[1,2,256]{2,1,0:T(2,128)S(1)} %bitcast.922), channel_id=1, source_target_pairs={{0,16},{16,32},{32,48},{48,64},{64,80},{80,96},{96,112},{112,128},... | collective-permute-start | bytes 6152 | tf_op jit(solution)/shard_map/ppermute | solution.py:25
  143.2 186.0 %collective-permute-start.1 = (f32[1,2,256]{2,1,0:T(2,128)S(1)}, f32[1,2,256]{2,1,0:T(2,128)S(1)}, u32[]{:S(2)}, u32[]{:S(2)}) collective-permute-start(f32[1,2,256]{2,1,0:T(2,128)S(1)} %bitcast.923), channel_id=1, source_target_pairs={{16,0},{32,16},{48,32},{64,48},{80,64},{96,80},{112,96},{128,112},... | collective-permute-start | bytes 6152 | tf_op jit(solution)/shard_map/ppermute | solution.py:26
  145.2 192.7 %collective-permute-start.4 = (f32[2,768]{1,0:T(2,128)S(1)}, f32[2,768]{1,0:T(2,128)S(1)}, u32[]{:S(2)}, u32[]{:S(2)}) collective-permute-start(f32[2,768]{1,0:T(2,128)S(1)} %get-tuple-element.600), channel_id=1, source_target_pairs={{0,8},{1,9},{2,10},{3,11},{4,12},{5,13},{6,14},{7,15},{8,0},{9,1},... | collective-permute-start | bytes 18440 | tf_op jit(solution)/shard_map/ppermute | solution.py:15
  152.5 525.3 %collective-permute-start.5 = (f32[768,768]{1,0:T(8,128)}, f32[768,768]{1,0:T(8,128)}, u32[]{:S(2)}, u32[]{:S(2)}) collective-permute-start(f32[768,768]{1,0:T(8,128)} %get-tuple-element.1222), channel_id=1, source_target_pairs={{0,8},{1,9},{2,10},{3,11},{4,12},{5,13},{6,14},{7,15},{8,0},{9,1},... | collective-permute-start | bytes 7077896 | tf_op jit(solution)/shard_map/ppermute | solution.py:15
  681.2 621.6 %collective-permute-start.6 = (f32[768,768]{0,1:T(8,128)}, f32[768,768]{0,1:T(8,128)}, u32[]{:S(2)}, u32[]{:S(2)}) collective-permute-start(f32[768,768]{0,1:T(8,128)} %get-tuple-element.317), channel_id=1, source_target_pairs={{0,8},{1,9},{2,10},{3,11},{4,12},{5,13},{6,14},{7,15},{8,0},{9,1},... | collective-permute-start | bytes 7077896 | tf_op jit(solution)/shard_map/ppermute | solution.py:15
  1311.9 6.4 collective-permute-start.8
  1318.4 12.8 collective-permute-start.9
  1320.3 11.6 collective-permute-start.10
  1479.1 6.1 collective-permute-start.11
  1483.2 6.4 collective-permute-start.12
  1505.3 6.4 collective-permute-start.16
  1657.4 6.6 collective-permute-start.19
  1662.0 6.4 collective-permute-start.20
  1758.8 5.7 collective-permute-start.23
  1762.5 6.4 collective-permute-start.24
  1913.9 6.3 collective-permute-start.27
  1918.2 6.4 collective-permute-start.28
  1924.7 6.1 collective-permute-start.29
  2015.1 5.7 collective-permute-start.31
  2018.8 6.4 collective-permute-start.32
  2025.2 6.2 collective-permute-start.33
  2170.0 6.9 collective-permute-start.35
  2174.3 6.4 collective-permute-start.36
  2180.7 7.0 collective-permute-start.37
  (24 other events, 702.8 us)
where the time goes:
time: 2200 us; the launch traced here: 2190 us
  other arithmetic  759 us (34%)
  blocking collectives  738 us (34%)
  local copies, waits for them, and re-layouts  288 us (13%)
  starting transfers between devices  200 us (9%)
  matrix products  122 us (6%)
  waiting for transfers between devices  54.6 us (2%)
    another operation x48, other arithmetic, lower_solve(): lax.linalg.triangular_solve(panel_matrix, right_side, left_side=True, low...  616 us
    psum x5, blocking collectives, global_sum(): return lax.psum(partial_value, ('group', 'member'))  375 us
    all_gather x5, blocking collectives, gather_coarse(): lax.all_gather(local_coarse.reshape(1, -1), ('group', 'member'), axis=0,...  364 us
    another operation x192, local copies, waits for them, and re-layouts, lower_solve(): lax.linalg.triangular_solve(panel_matrix, right_side, left_side=True, low...  155 us
    another operation x12, other arithmetic, upper_solve(): lax.linalg.triangular_solve(panel_matrix, right_side, left_side=True, low...  123 us
    ppermute x3, starting transfers between devices, from_partner(): return lax.ppermute(value, axis, pairs)  90.3 us
    gather x3, local copies, waits for them, and re-layouts, shards(): jnp.take_along_axis(mode_table, jnp.broadcast_to(dof_map[0][:, None, :],...  71.1 us
    ppermute x18, starting transfers between devices, padded(): before = lax.ppermute(last, axis, up)  63.6 us
  transfers between devices with their start and end apart: 39, of which 17 were waited for; matrix products, arithmetic and copies ran while one was open for 47% of the time, Pallas kernels for 0%

commit v1 on v0

--- a/solution.py
+++ b/solution.py
@@ -195,7 +195,15 @@
         return lax.psum(partial_value, ("group", "member"))
 
     def gather_coarse(local_coarse):
-        return lax.all_gather(local_coarse.reshape(1, -1), ("group", "member"), axis=0, tiled=True)
+        return jnp.concatenate(
+            lax.all_to_all(
+                jnp.stack(lax.axis_size(("group", "member")) * [local_coarse.reshape(1, -1)]),
+                ("group", "member"),
+                0,
+                0,
+            ),
+            0,
+        )
 
     def coarse_of(values):
         return jnp.einsum("laj,lj->la", rigid_rows, values, precision=highest)

time: 2200 us -> 1950 us (0.89)
  blocking collectives: 738 us -> 407 us
  starting transfers between devices: 200 us -> 253 us
    all_gather x5 -> x0, blocking collectives: 364 us -> none  [gather_coarse(): lax.all_gather(local_coarse.reshape(1, -1), ('group', 'member'), axis=0,...]
    ppermute x18, starting transfers between devices: 46.3 us -> 138 us  [padded(): after = lax.ppermute(leading, axis, down)]
    ppermute x3, starting transfers between devices: 90.3 us -> 7.51 us  [from_partner(): return lax.ppermute(value, axis, pairs)]
    all_to_all x0 -> x2, blocking collectives: none -> 41.2 us  [gather_coarse(): lax.all_to_all(jnp.stack(lax.axis_size(('group', 'member')) * [local_coar...]
    all_to_all x0 -> x3, starting transfers between devices: none -> 34.7 us  [gather_coarse(): lax.all_to_all(jnp.stack(lax.axis_size(('group', 'member')) * [local_coar...]
  transfers between devices with their start and end apart: 39 -> 42, of which waited for: 17 -> 20; matrix products, arithmetic and copies ran while one was open for 47% -> 58% of each run, Pallas kernels for 0% -> 0%
where the time goes in v1:
time: 1950 us; the launch traced here: 1940 us
  other arithmetic  765 us (39%)
  blocking collectives  407 us (21%)
  local copies, waits for them, and re-layouts  291 us (15%)
  starting transfers between devices  253 us (13%)
  matrix products  122 us (6%)
  waiting for transfers between devices  76.5 us (4%)
    another operation x48, other arithmetic, lower_solve(): lax.linalg.triangular_solve(panel_matrix, right_side, left_side=True, low...  616 us
    psum x5, blocking collectives, global_sum(): return lax.psum(partial_value, ('group', 'member'))  366 us
    another operation x192, local copies, waits for them, and re-layouts, lower_solve(): lax.linalg.triangular_solve(panel_matrix, right_side, left_side=True, low...  157 us
    ppermute x18, starting transfers between devices, padded(): after = lax.ppermute(leading, axis, down)  138 us
    another operation x12, other arithmetic, upper_solve(): lax.linalg.triangular_solve(panel_matrix, right_side, left_side=True, low...  123 us
    ppermute x18, starting transfers between devices, padded(): before = lax.ppermute(last, axis, up)  72.6 us
    gather x3, local copies, waits for them, and re-layouts, shards(): jnp.take_along_axis(mode_table, jnp.broadcast_to(dof_map[0][:, None, :],...  71.1 us
    ppermute x18, waiting for transfers between devices, padded(): after = lax.ppermute(leading, axis, down)  57.6 us
  transfers between devices with their start and end apart: 42, of which 20 were waited for; matrix products, arithmetic and copies ran while one was open for 58% of the time, Pallas kernels for 0%

profile of v1, /device:TPU:15, one launch (start us, length us, event | category | flops | bytes accessed | tf_op | source)
XLA Modules:
  0.0 1942.8 jit_solution(9692408481388661312)
XLA Ops:
  30.7 71.1 %gather_fusion = f32[9216]{0:T(1024)S(1)} fusion(f32[2,6,768]{2,1,0:T(8,128)S(1)} %stack.159, s32[9216]{0:T(1024)S(1)} %reshape.398), kind=kCustom, calls=%fused_computation | custom fusion | bytes 184320 | tf_op jit(solution)/shard_map/jit(take_along_axis)/gather | solution.py:158
  125.4 117.9 %custom-call.8 = f32[2,6,128,128]{2,3,1,0:T(8,128)S(1)} custom-call(f32[2,6,128,128]{3,2,1,0:T(8,128)S(1)} %bitcast.1018), custom_call_target="InvertDiagBlocksLowerTriangular" | custom-call | tf_op jit(solution)/shard_map/vmap()/triangular_solve | solution.py:60
  289.4 331.0 %while.88 = (s32[]{:T(128)}, f32[768,768]{1,0:T(8,128)}, s32[]{:T(128)}, f32[768]{0:T(1024)}, f32[768,768]{1,0:T(8,128)}, /*index=5*/s32[]{:T(128)}, s32[]{:T(128)}, s32[]{:T(128)}, s32[]{:T(128)}, s32[]{:T(128)}) while((s32[]{:T(128)}, f32[768,768]{1,0:T(8,128)}, s32[]{:T(128)}, f32[768]{0:T(1024)}, f32[768,768]{1,0:T(8,128)}, ...), condition=%wide.region_12.14_spmd.clone, body=%wide.region_11.13_spmd.clone.sunk | while | flops 530268544 | bytes 10424716 | solution.py:78
  308.3 59.8 %custom-call.57 = f32[6,128,128]{1,2,0:T(8,128)S(1)} custom-call(f32[6,128,128]{2,1,0:T(8,128)} %get-tuple-element.1070), custom_call_target="InvertDiagBlocksLowerTriangular" | custom-call | tf_op jit(solution)/shard_map/while/body/triangular_solve/custom-call.1 | solution.py:56
  391.0 59.8 %custom-call.57 = f32[6,128,128]{1,2,0:T(8,128)S(1)} custom-call(f32[6,128,128]{2,1,0:T(8,128)} %get-tuple-element.1070), custom_call_target="InvertDiagBlocksLowerTriangular" | custom-call | tf_op jit(solution)/shard_map/while/body/triangular_solve/custom-call.1 | solution.py:56
  473.7 59.8 %custom-call.57 = f32[6,128,128]{1,2,0:T(8,128)S(1)} custom-call(f32[6,128,128]{2,1,0:T(8,128)} %get-tuple-element.1070), custom_call_target="InvertDiagBlocksLowerTriangular" | custom-call | tf_op jit(solution)/shard_map/while/body/triangular_solve/custom-call.1 | solution.py:56
  556.4 59.8 %custom-call.57 = f32[6,128,128]{1,2,0:T(8,128)S(1)} custom-call(f32[6,128,128]{2,1,0:T(8,128)} %get-tuple-element.1070), custom_call_target="InvertDiagBlocksLowerTriangular" | custom-call | tf_op jit(solution)/shard_map/while/body/triangular_solve/custom-call.1 | solution.py:56
  622.0 498.4 %while.84 = (s32[]{:T(128)}, f32[768,768]{1,0:T(8,128)}, s32[]{:T(128)}, f32[768]{0:T(1024)}, f32[768,768]{1,0:T(8,128)}, /*index=5*/s32[]{:T(128)}, s32[]{:T(128)}, s32[]{:T(128)}, s32[]{:T(128)}, s32[]{:T(128)}) while((s32[]{:T(128)}, f32[768,768]{1,0:T(8,128)}, s32[]{:T(128)}, f32[768]{0:T(1024)}, f32[768,768]{1,0:T(8,128)}, ...), condition=%wide.region_2.4_spmd.clone, body=%wide.region_1.3_spmd.clone.sunk | while | flops 530268544 | bytes 10424716 | solution.py:78
  641.0 59.8 %custom-call.51 = f32[6,128,128]{1,2,0:T(8,128)S(1)} custom-call(f32[6,128,128]{2,1,0:T(8,128)} %get-tuple-element.1024), custom_call_target="InvertDiagBlocksLowerTriangular" | custom-call | tf_op jit(solution)/shard_map/while/body/triangular_solve/custom-call.1 | solution.py:56
  723.9 59.8 %custom-call.51 = f32[6,128,128]{1,2,0:T(8,128)S(1)} custom-call(f32[6,128,128]{2,1,0:T(8,128)} %get-tuple-element.1024), custom_call_target="InvertDiagBlocksLowerTriangular" | custom-call | tf_op jit(solution)/shard_map/while/body/triangular_solve/custom-call.1 | solution.py:56
  806.9 59.8 %custom-call.51 = f32[6,128,128]{1,2,0:T(8,128)S(1)} custom-call(f32[6,128,128]{2,1,0:T(8,128)} %get-tuple-element.1024), custom_call_target="InvertDiagBlocksLowerTriangular" | custom-call | tf_op jit(solution)/shard_map/while/body/triangular_solve/custom-call.1 | solution.py:56
  889.9 59.8 %custom-call.51 = f32[6,128,128]{1,2,0:T(8,128)S(1)} custom-call(f32[6,128,128]{2,1,0:T(8,128)} %get-tuple-element.1024), custom_call_target="InvertDiagBlocksLowerTriangular" | custom-call | tf_op jit(solution)/shard_map/while/body/triangular_solve/custom-call.1 | solution.py:56
  972.9 59.8 %custom-call.51 = f32[6,128,128]{1,2,0:T(8,128)S(1)} custom-call(f32[6,128,128]{2,1,0:T(8,128)} %get-tuple-element.1024), custom_call_target="InvertDiagBlocksLowerTriangular" | custom-call | tf_op jit(solution)/shard_map/while/body/triangular_solve/custom-call.1 | solution.py:56
  1055.8 59.8 %custom-call.51 = f32[6,128,128]{1,2,0:T(8,128)S(1)} custom-call(f32[6,128,128]{2,1,0:T(8,128)} %get-tuple-element.1024), custom_call_target="InvertDiagBlocksLowerTriangular" | custom-call | tf_op jit(solution)/shard_map/while/body/triangular_solve/custom-call.1 | solution.py:56
  1135.6 23.8 %while.79 = (s32[]{:T(128)}, f32[768,768]{0,1:T(8,128)S(1)}, s32[]{:T(128)}, f32[768,768]{1,0:T(8,128)}, s32[]{:T(128)}, /*index=5*/s32[]{:T(128)}, s32[]{:T(128)}, s32[]{:T(128)}) while((s32[]{:T(128)}, f32[768,768]{0,1:T(8,128)S(1)}, s32[]{:T(128)}, f32[768,768]{1,0:T(8,128)}, s32[]{:T(128)}, /*index=5*/s32[]{:T(128)}, s32[]{:T(128)}, ...), condition=%wide.region_4.6_spmd, body=%wide.region_3.5_spmd.sunk | while | flops 905969664 | bytes 3146883 | solution.py:93
  1184.3 84.4 %collective-permute-start.3 = (f32[3,1,256]{2,1,0:T(1,128)S(1)}, f32[3,1,256]{2,1,0:T(1,128)S(1)}, u32[]{:S(2)}, u32[]{:S(2)}) collective-permute-start(f32[3,1,256]{2,1,0:T(1,128)S(1)} %get-tuple-element.619), channel_id=1, source_target_pairs={{1,0},{2,1},{3,2},{4,3},{5,4},{6,5},{7,6},{8,7},{9,8},{10,9},{11,1... | collective-permute-start | bytes 9224 | tf_op jit(solution)/shard_map/ppermute | solution.py:26
  1286.5 19.8 %collective-permute-start.10 = (f32[3,1,256]{2,1,0:T(1,128)S(1)}, f32[3,1,256]{2,1,0:T(1,128)S(1)}, u32[]{:S(2)}, u32[]{:S(2)}) collective-permute-start(f32[3,1,256]{2,1,0:T(1,128)S(1)} %get-tuple-element.617), channel_id=1, source_target_pairs={{1,0},{2,1},{3,2},{4,3},{5,4},{6,5},{7,6},{8,7},{9,8},{10,9},{11,1... | collective-permute-start | bytes 9224 | tf_op jit(solution)/shard_map/ppermute | solution.py:26
  1376.0 73.2 %all-reduce = (f32[]{:T(128)}, f32[]{:T(128)}) all-reduce(f32[]{:T(128)} %get-tuple-element.439, f32[]{:T(128)} %get-tuple-element.438), channel_id=1, replica_groups=mesh['group'=16,'member'=16] {'group','member'}, use_global_device_ids=true, to_apply=%region_16.18 | all-reduce | flops 2 | bytes 16 | tf_op jit(solution)/shard_map/psum | solution.py:195
  1450.9 20.6 %all_to_all.25 = f32[256,1,12]{2,1,0:T(1,128)S(1)} all-to-all(f32[256,1,12]{2,1,0:T(1,128)S(1)} %stack.185), channel_id=1, replica_groups=mesh['group'=16,'member'=16] {'group','member'}, dimensions={0} | all-to-all | bytes 24576 | tf_op jit(solution)/shard_map/all_to_all | solution.py:199
  1496.9 72.6 %psum.44 = f32[]{:T(128)} all-reduce(f32[]{:T(128)} %fusion.217), channel_id=1, replica_groups=mesh['group'=16,'member'=16] {'group','member'}, use_global_device_ids=true, to_apply=%region_20.22 | all-reduce | flops 1 | bytes 8 | tf_op jit(solution)/shard_map/psum | solution.py:195
  1598.0 73.6 %psum.45 = f32[]{:T(128)} all-reduce(f32[]{:T(128)} %multiply_reduce_fusion.1), channel_id=1, replica_groups=mesh['group'=16,'member'=16] {'group','member'}, use_global_device_ids=true, to_apply=%region_22.24 | all-reduce | flops 1 | bytes 8 | tf_op jit(solution)/shard_map/psum | solution.py:195
  1673.3 20.6 %all_to_all.26 = f32[256,1,12]{2,1,0:T(1,128)S(1)} all-to-all(f32[256,1,12]{2,1,0:T(1,128)S(1)} %stack.192), channel_id=1, replica_groups=mesh['group'=16,'member'=16] {'group','member'}, dimensions={0} | all-to-all | bytes 24576 | tf_op jit(solution)/shard_map/all_to_all | solution.py:199
  1719.2 72.6 %psum.46 = f32[]{:T(128)} all-reduce(f32[]{:T(128)} %get-tuple-element.530), channel_id=1, replica_groups=mesh['group'=16,'member'=16] {'group','member'}, use_global_device_ids=true, to_apply=%region_24.26 | all-reduce | flops 1 | bytes 8 | tf_op jit(solution)/shard_map/psum | solution.py:195
  1820.4 73.6 %psum.47 = f32[]{:T(128)} all-reduce(f32[]{:T(128)} %multiply_reduce_fusion), channel_id=1, replica_groups=mesh['group'=16,'member'=16] {'group','member'}, use_global_device_ids=true, to_apply=%region_26.28 | all-reduce | flops 1 | bytes 8 | tf_op jit(solution)/shard_map/psum | solution.py:195
  (801 shorter events, 806.1 us)
Async XLA Ops:
  1.5 274.6 %collective-permute-start.4 = (f32[2,768]{1,0:T(2,128)S(1)}, f32[2,768]{1,0:T(2,128)S(1)}, u32[]{:S(2)}, u32[]{:S(2)}) collective-permute-start(f32[2,768]{1,0:T(2,128)S(1)} %get-tuple-element.600), channel_id=1, source_target_pairs={{0,8},{1,9},{2,10},{3,11},{4,12},{5,13},{6,14},{7,15},{8,0},{9,1},... | collective-permute-start | bytes 18440 | tf_op jit(solution)/shard_map/ppermute | solution.py:15
  13.3 1151.4 %collective-permute-start.5 = (f32[768,768]{1,0:T(8,128)}, f32[768,768]{1,0:T(8,128)}, u32[]{:S(2)}, u32[]{:S(2)}) collective-permute-start(f32[768,768]{1,0:T(8,128)} %get-tuple-element.1222), channel_id=1, source_target_pairs={{0,8},{1,9},{2,10},{3,11},{4,12},{5,13},{6,14},{7,15},{8,0},{9,1},... | collective-permute-start | bytes 7077896 | tf_op jit(solution)/shard_map/ppermute | solution.py:15
  15.3 1146.1 %all-to-all-start = ((f32[256,1,12]{2,1,0:T(1,128)}), f32[256,1,12]{2,1,0:T(1,128)S(1)}, u32[]{:S(2)}, u32[]{:S(2)}) async-start(f32[256,1,12]{2,1,0:T(1,128)} %stack.160), calls=%async_computation | async-start | bytes 262144 | tf_op jit(solution)/shard_map/all_to_all | solution.py:199
  1166.6 103.8 %collective-permute-start.6 = (f32[768,768]{0,1:T(8,128)S(1)}, f32[768,768]{0,1:T(8,128)S(1)}, u32[]{:S(2)}, u32[]{:S(2)}) collective-permute-start(f32[768,768]{0,1:T(8,128)S(1)} %get-tuple-element.317), channel_id=1, source_target_pairs={{0,8},{1,9},{2,10},{3,11},{4,12},{5,13},{6,14},{7,15},{8,0},{9,1},... | collective-permute-start | bytes 7077896 | tf_op jit(solution)/shard_map/ppermute | solution.py:15
  1168.1 9.5 collective-permute-start
  1175.6 6.7 collective-permute-start.1
  1182.3 86.5 %collective-permute-start.2 = (f32[3,1,256]{2,1,0:T(1,128)S(1)}, f32[3,1,256]{2,1,0:T(1,128)S(1)}, u32[]{:S(2)}, u32[]{:S(2)}) collective-permute-start(f32[3,1,256]{2,1,0:T(1,128)S(1)} %get-tuple-element.618), channel_id=1, source_target_pairs={{0,1},{1,2},{2,3},{3,4},{4,5},{5,6},{6,7},{7,8},{8,9},{9,10},{10,1... | collective-permute-start | bytes 9224 | tf_op jit(solution)/shard_map/ppermute | solution.py:25
  1184.3 85.2 %collective-permute-start.3 = (f32[3,1,256]{2,1,0:T(1,128)S(1)}, f32[3,1,256]{2,1,0:T(1,128)S(1)}, u32[]{:S(2)}, u32[]{:S(2)}) collective-permute-start(f32[3,1,256]{2,1,0:T(1,128)S(1)} %get-tuple-element.619), channel_id=1, source_target_pairs={{1,0},{2,1},{3,2},{4,3},{5,4},{6,5},{7,6},{8,7},{9,8},{10,9},{11,1... | collective-permute-start | bytes 9224 | tf_op jit(solution)/shard_map/ppermute | solution.py:26
  1278.1 6.4 collective-permute-start.8
  1284.6 21.8 %collective-permute-start.9 = (f32[3,1,256]{2,1,0:T(1,128)S(1)}, f32[3,1,256]{2,1,0:T(1,128)S(1)}, u32[]{:S(2)}, u32[]{:S(2)}) collective-permute-start(f32[3,1,256]{2,1,0:T(1,128)S(1)} %get-tuple-element.616), channel_id=1, source_target_pairs={{0,1},{1,2},{2,3},{3,4},{4,5},{5,6},{6,7},{7,8},{8,9},{9,10},{10,1... | collective-permute-start | bytes 9224 | tf_op jit(solution)/shard_map/ppermute | solution.py:25
  1286.5 20.6 %collective-permute-start.10 = (f32[3,1,256]{2,1,0:T(1,128)S(1)}, f32[3,1,256]{2,1,0:T(1,128)S(1)}, u32[]{:S(2)}, u32[]{:S(2)}) collective-permute-start(f32[3,1,256]{2,1,0:T(1,128)S(1)} %get-tuple-element.617), channel_id=1, source_target_pairs={{1,0},{2,1},{3,2},{4,3},{5,4},{6,5},{7,6},{8,7},{9,8},{10,9},{11,1... | collective-permute-start | bytes 9224 | tf_op jit(solution)/shard_map/ppermute | solution.py:26
  1308.9 19.3 all-to-all-start.1
  1335.9 6.4 collective-permute-start.12
  1342.4 7.1 collective-permute-start.13
  1360.0 6.4 collective-permute-start.16
  1479.3 6.4 collective-permute-start.20
  1485.7 6.9 collective-permute-start.21
  1579.6 6.4 collective-permute-start.24
  1586.0 7.7 collective-permute-start.25
  1701.6 6.4 collective-permute-start.28
  1708.1 6.9 collective-permute-start.29
  1808.4 7.7 collective-permute-start.33
  1896.4 20.7 %all-to-all-start.4 = ((f32[256,1,12]{2,1,0:T(1,128)}), f32[256,1,12]{2,1,0:T(1,128)S(1)}, u32[]{:S(2)}, u32[]{:S(2)}) async-start(f32[256,1,12]{2,1,0:T(1,128)} %stack.199), calls=%async_computation.4 | async-start | bytes 262144 | tf_op jit(solution)/shard_map/all_to_all | solution.py:199
  1931.3 6.9 collective-permute-start.37
  (33 other events, 336.5 us)
